TPU v7x, 32 devices: a whole 2x2x4 slice. The times are simulated.
32 devices in a mesh: seq: 4 (over y, core), fsdp: 2 (over x), dp: 4 (over z).
Axes of the slice: x: 2, y: 2, z: 4, core: 2. Of those that a mesh axis runs over, the one named last changes fastest.
Arguments:
- queries: bfloat16 [8, 1024, 4096], P(('fsdp', 'dp'), 'seq'), may hold values from -160 to 160
- hidden: bfloat16 [8, 1024, 8192], P(('fsdp', 'dp'), 'seq'), may hold values from -8 to 8
- key_weight: bfloat16 [8192, 512], P('fsdp'), may hold values from -1 to 1
- doc_lengths: int32 [8, 8], P(('fsdp', 'dp')), may hold values from 1 to 256, 1024 in all within a row
- entropy_cot: bfloat16 [8, 1024, 32], P(('fsdp', 'dp'), 'seq'), may hold values from -600 to 600
Outputs:
- entropy: float32 [8, 1024, 32], P(('fsdp', 'dp'), 'seq')
- grad_queries: bfloat16 [8, 1024, 4096], P(('fsdp', 'dp'), 'seq')
- grad_key_weight: bfloat16 [8192, 512], P('fsdp')
Inputs may be any that keep to these rules, and one draw needn't show every extreme that they name: `doc_lengths`: each sequence's 8 documents are packed in order, their lengths sum to 1024, and the longest is exactly 256.
All inputs are finite; a program needn't handle non-finite values.
Results may differ from a plain program's by a relative error of at most 0.0088.
Values may be sent and summed in bfloat16 or wider, within the bound.
A program may use at most 128 MiB of HBM per device.

v0:
```python
import jax
import jax.numpy as jnp
from jax import lax
from jax.sharding import PartitionSpec as P

QH = 32
KVH = 4
HD = 128


def from_behind(shard, axis, by):
    length = lax.axis_size(axis)
    pairs = [(i, i + by) for i in range(length) if 0 <= i + by < length]
    return lax.ppermute(shard, axis, pairs)


def document_index(lengths, seq_len):
    ends = jnp.cumsum(lengths)
    position = jnp.arange(seq_len, dtype=jnp.int32)
    return jnp.sum((ends[None, :] <= position[:, None]).astype(jnp.int32), axis=1)


def attend(queries, key_rows, cotangent, doc_index, anchor, doc_len):
    row_count, key_heads, group_size, head_size = queries.shape
    full_len = key_rows.shape[0]
    block_rows = min(512, row_count)
    window = block_rows + doc_len
    factor = head_size ** (-0.5)
    keys_padded = jnp.concatenate(
        [jnp.zeros((doc_len, key_heads, head_size), key_rows.dtype), key_rows], axis=0
    )
    index_padded = jnp.concatenate([jnp.full((doc_len,), -1, jnp.int32), doc_index], axis=0)

    def one_block(step_index, state_now):
        entropy, grad_query, grad_key = state_now
        row_start = (step_index * block_rows).astype(jnp.int32)
        position = anchor + row_start
        weight_block = cotangent.astype(jnp.float32)
        key_block = lax.dynamic_slice_in_dim(keys_padded, position, window, 0)
        key_docs = lax.dynamic_slice_in_dim(index_padded, position, window, 0)
        query_docs = lax.dynamic_slice_in_dim(doc_index, position, block_rows, 0)
        query_pos = position + jnp.arange(block_rows, dtype=jnp.int32)
        key_pos = position - doc_len + jnp.arange(window, dtype=jnp.int32)
        visible = (query_docs[:, None] == key_docs[None, :]) & (
            key_pos[None, :] <= query_pos[:, None]
        )
        scores = (
            jnp.einsum("rkgd,wkd->kgrw", queries, key_block, preferred_element_type=jnp.float32)
            * factor
        )
        scores = jnp.where(visible, scores, -1e30)
        row_max = jnp.max(scores, axis=-1, keepdims=True)
        powers = jnp.exp(scores - row_max)
        denominator = jnp.sum(powers, axis=-1, keepdims=True)
        probability = powers / denominator
        mean_score = jnp.sum(jnp.where(visible, probability * scores, 0.0), axis=-1, keepdims=True)
        block_entropy = (row_max + jnp.log(denominator) - mean_score)[..., 0]
        row_weight = jnp.transpose(weight_block, (1, 2, 0))[..., None]
        slope = jnp.where(visible, row_weight * probability * (mean_score - scores), 0.0).astype(
            jnp.bfloat16
        )
        query_part = (
            jnp.einsum("kgrw,wkd->rkgd", slope, key_block, preferred_element_type=jnp.float32)
            * factor
        )
        key_part = (
            jnp.einsum("kgrw,rkgd->wkd", slope, queries, preferred_element_type=jnp.float32)
            * factor
        )
        entropy = jnp.transpose(block_entropy, (2, 0, 1))
        grad_query = query_part
        previous = lax.dynamic_slice_in_dim(grad_key, position, window, 0)
        grad_key = lax.dynamic_update_slice_in_dim(grad_key, previous + key_part, position, 0)
        return (entropy, grad_query, grad_key)

    initial = (
        jnp.zeros((row_count, key_heads, group_size), jnp.float32),
        jnp.zeros((row_count, key_heads, group_size, head_size), jnp.float32),
        jnp.zeros((full_len + doc_len, key_heads, head_size), jnp.float32),
    )
    entropy, grad_query, grad_key = lax.fori_loop(0, row_count // block_rows, one_block, initial)
    return (entropy, grad_query, grad_key[doc_len:])


def per_head(query_four, key_rows, cot_three, doc_index, anchor, doc_len):
    outcome = [
        attend(
            query_four[:, head_index : head_index + 1],
            key_rows[:, head_index : head_index + 1],
            cot_three[:, head_index : head_index + 1],
            doc_index,
            anchor,
            doc_len,
        )
        for head_index in range(query_four.shape[1])
    ]
    entropy = jnp.concatenate([item_set[0] for item_set in outcome], axis=1)
    grad_query = jnp.concatenate([item_set[1] for item_set in outcome], axis=1)
    grad_key = jnp.concatenate([item_set[2] for item_set in outcome], axis=1)
    return (entropy, grad_query, grad_key)


def shards(queries, hidden, key_weight, doc_lengths, entropy_cot):
    tokens = hidden[0]
    local_rows = tokens.shape[0]
    seq_parts = lax.axis_size("seq")
    seq_len = local_rows * seq_parts
    group_size = QH // KVH
    doc_index = document_index(doc_lengths[0], seq_len)
    columns = tokens
    key_local = jnp.dot(
        columns,
        lax.all_gather(key_weight, "fsdp", axis=0, tiled=True),
        preferred_element_type=jnp.float32,
    ).astype(jnp.bfloat16)
    query_local = queries[0]
    cot_local = entropy_cot[0]
    key_prev = from_behind(key_local, "seq", 1)
    device_pos = lax.axis_index("seq")
    start = device_pos * local_rows
    prev_index = lax.dynamic_slice_in_dim(
        doc_index, jnp.maximum(start - local_rows, 0), local_rows, 0
    )
    prev_index = jnp.where(device_pos > 0, prev_index, -1)
    own_index = lax.dynamic_slice_in_dim(doc_index, start, local_rows, 0)
    ext_index = jnp.concatenate([prev_index, own_index], axis=0)
    ext_keys = jnp.concatenate([key_prev, key_local], axis=0).reshape(2 * local_rows, KVH, HD)
    entropy_heads, grad_heads, key_heads_ext = per_head(
        query_local.reshape(local_rows, KVH, group_size, HD),
        ext_keys,
        cot_local.reshape(local_rows, KVH, group_size),
        ext_index,
        local_rows,
        local_rows,
    )
    entropy_local = entropy_heads.reshape(local_rows, QH)
    grad_local = grad_heads.reshape(local_rows, QH * HD)
    key_ext = key_heads_ext.reshape(2 * local_rows, KVH * HD)
    returned = from_behind(key_ext[:local_rows], "seq", -1)
    key_grad = key_ext[local_rows:] + returned
    key_grad_low = key_grad.astype(jnp.bfloat16)
    columns = tokens
    term_rows = lax.psum_scatter(
        lax.dot_general(
            columns, key_grad_low, (((0,), (0,)), ((), ())), preferred_element_type=jnp.float32
        ),
        "fsdp",
        scatter_dimension=0,
        tiled=True,
    )
    summed = lax.psum(term_rows, ("seq", "dp"))
    norm_factor = (seq_len * lax.axis_size("fsdp") * lax.axis_size("dp")) ** (-0.5)
    weight_grad = (summed * norm_factor).astype(jnp.bfloat16)
    return (
        entropy_local.reshape(1, local_rows, QH),
        grad_local.astype(jnp.bfloat16).reshape(1, local_rows, QH * HD),
        weight_grad,
    )


def solution(mesh):
    return jax.shard_map(
        shards,
        mesh=mesh,
        in_specs=(
            P(("fsdp", "dp"), "seq", None),
            P(("fsdp", "dp"), "seq", None),
            P("fsdp", None),
            P(("fsdp", "dp"), None),
            P(("fsdp", "dp"), "seq", None),
        ),
        out_specs=(P(("fsdp", "dp"), "seq", None), P(("fsdp", "dp"), "seq", None), P("fsdp", None)),
        check_vma=False,
    )
```

profile of v0, /device:TPU:0, one launch (start us, length us, event | category | flops | bytes accessed | tf_op | source)
XLA Modules:
  0.0 553.6 jit_solution(1819505736635313049)
XLA Ops:
  7.2 0.0 all-gather.2.cloned.1.call-start
  7.2 0.7 all-gather.2.cloned.1.call-update
  7.9 0.0 reduce-scatter.2.cloned.1.call-start
  8.0 0.2 reduce-window.8
  8.2 0.1 convert_reduce_fusion
  8.3 0.1 dynamic-slice_select_fusion
  8.3 0.6 convert_bitcast_fusion.3
  8.9 107.3 %all-gather.2.cloned.1.call-done = bf16[8192,512]{1,0:T(8,128)(2,1)} async-done(((bf16[4096,512]{1,0:T(8,128)(2,1)}), bf16[8192,512]{1,0:T(8,128)(2,1)}) %all-gather.2.cloned.1.call-update) | async-done | bytes 8388624 | tf_op jit(solution)/shard_map/all_gather | solution.py:113
  116.3 7.0 %fusion.67 = bf16[256,512]{1,0:T(8,128)(2,1)S(1)} fusion(bf16[8192,512]{1,0:T(8,128)(2,1)} %all-gather.2.cloned.1.call-done, bf16[1,256,8192]{2,1,0:T(8,128)(2,1)} %param.6), kind=kOutput, calls=%fused_computation.62 | convolution fusion | flops 2147614720 | bytes 12845056 | tf_op jit(solution)/shard_map/dot_general | solution.py:111
  123.3 1.6 collective-permute-start
  124.9 3.3 copy.58
  128.2 0.1 fusion.107
  128.3 0.0 collective-permute-done
  128.4 0.1 reshape.341
  128.5 0.8 fusion.113
  129.2 0.0 copy-start.8
  129.3 0.7 fusion.110
  130.0 0.0 copy-start.2
  130.0 0.7 fusion.111
  130.7 0.0 copy-start
  130.7 0.8 fusion.11
  131.5 0.9 fusion.4
  132.4 3.6 select_reduce_fusion.3
  136.0 2.6 fusion.6
  138.7 0.0 copy-start.22
  138.7 0.0 copy-start.19
  138.7 0.0 copy-start.13
  138.7 0.0 copy-start.43
  138.7 4.5 select_reduce_fusion.2
  143.2 0.0 copy-start.27
  143.3 1.8 fusion.97
  145.2 1.8 fusion.91
  147.0 0.0 copy-done
  147.0 0.0 copy-done.13
  147.0 1.8 fusion.85
  148.9 1.8 fusion.103
  150.7 0.0 copy-start.7
  150.7 0.1 pad_maximum_fusion.1
  150.8 0.1 fusion.112
  150.9 1.6 collective-permute-start.1
  152.5 3.9 collective-permute-done.1
  156.4 0.1 fusion.106
  156.5 8.1 %convolution_bitcast_fusion = f32[8192,512]{0,1:T(8,128)} fusion(bf16[256,512]{0,1:T(8,128)(2,1)S(1)} %fusion.106, bf16[1,256,8192]{2,1,0:T(8,128)(2,1)S(1)} %copy-done.7), kind=kOutput, calls=%fused_computation | convolution fusion | flops 2147483648 | bytes 21233664 | tf_op jit(solution)/shard_map/dot_general | solution.py:144
  164.6 0.0 reduce-scatter.2.cloned.1.call-update
  164.6 0.3 all-reduce.2.cloned.1.call-start
  164.8 195.6 %reduce-scatter.2.cloned.1.call-done = f32[4096,512]{0,1:T(8,128)} async-done(((f32[8192,512]{0,1:T(8,128)}), f32[4096,512]{0,1:T(8,128)}) %reduce-scatter.2.cloned.1.call-update) | async-done | bytes 8388624 | tf_op jit(solution)/shard_map/reduce_scatter | solution.py:143
  360.5 0.0 all-reduce.2.cloned.1.call-update
  360.5 0.9 copy-done.9
  361.5 4.1 fusion.58
  365.6 0.0 copy-done.3
  365.6 0.0 copy-start.1
  365.6 0.0 copy-start.28
  365.7 1.8 fusion.61
  367.4 0.4 copy-done.1
  367.9 1.8 fusion.64
  369.6 0.8 copy-done.5
  370.5 1.8 fusion.55
  372.3 0.0 copy-start.29
  372.3 0.3 pad_maximum_fusion
  372.6 2.9 copy.82
  375.6 0.6 maximum_bitcast_fusion
  376.2 158.1 %all-reduce.2.cloned.1.call-done = f32[4096,512]{0,1:T(8,128)} async-done(((f32[4096,512]{0,1:T(8,128)}), f32[4096,512]{0,1:T(8,128)}) %all-reduce.2.cloned.1.call-update) | async-done | bytes 8388624 | tf_op jit(solution)/shard_map/psum | solution.py:151
  534.3 6.4 %multiply_convert_fusion = bf16[4096,512]{0,1:T(8,128)(2,1)} fusion(f32[4096,512]{0,1:T(8,128)} %all-reduce.2.cloned.1.call-done), kind=kLoop, calls=%fused_computation.1 | loop fusion | flops 4194304 | bytes 12582912 | tf_op jit(solution)/shard_map/convert_element_type | solution.py:153
  540.7 6.4 %copy.83 = bf16[4096,512]{1,0:T(8,128)(2,1)} copy(bf16[4096,512]{0,1:T(8,128)(2,1)} %multiply_convert_fusion) | data formatting | bytes 8388608
  (84 shorter events, 0.2 us)
Async XLA Ops:
  7.2 0.8 copy-start.47
  7.2 1.2 copy-start.36
  7.2 109.1 %all-gather.2.cloned.1.call-start = ((), (), s32[]{:S(2)}) async-start(), calls=%async_computation.1 | async-start | bytes 12582912 | tf_op jit(solution)/shard_map/all_gather | solution.py:113
  7.9 352.5 %reduce-scatter.2.cloned.1.call-start = ((), (), s32[]{:S(2)}) async-start(), calls=%async_computation.2 | async-start | bytes 25165824 | tf_op jit(solution)/shard_map/reduce_scatter | solution.py:143
  123.3 5.0 collective-permute-start
  129.2 3.1 copy-start.8
  130.0 15.2 %copy-start.2 = (f32[512,256,8]{1,0,2:T(8,128)}, f32[512,256,8]{1,0,2:T(8,128)S(1)}, u32[]{:S(2)}) copy-start(f32[512,256,8]{1,0,2:T(8,128)S(1)} %fusion.110) | copy-start | bytes 12582916
  130.7 16.3 %copy-start = (f32[512,256,8]{1,0,2:T(8,128)}, f32[512,256,8]{1,0,2:T(8,128)S(1)}, u32[]{:S(2)}) copy-start(f32[512,256,8]{1,0,2:T(8,128)S(1)} %fusion.111) | copy-start | bytes 12582916
  131.5 17.4 %copy-start.4 = (f32[512,256,8]{1,0,2:T(8,128)}, f32[512,256,8]{1,0,2:T(8,128)S(1)}, u32[]{:S(2)}) copy-start(f32[512,256,8]{1,0,2:T(8,128)S(1)} %get-tuple-element.127) | copy-start | bytes 12582916
  132.4 16.5 %copy-start.25 = (f32[8,256]{1,0:T(8,128)}, f32[8,256]{1,0:T(8,128)S(1)}, u32[]{:S(2)}) copy-start(f32[8,256]{1,0:T(8,128)S(1)} %fusion.4) | copy-start | bytes 24580
  136.0 7.2 %copy-start.6 = (f32[512,256,8]{1,0,2:T(8,128)}, f32[512,256,8]{1,0,2:T(8,128)S(1)}, u32[]{:S(2)}) copy-start(f32[512,256,8]{1,0,2:T(8,128)S(1)} %get-tuple-element.128) | copy-start | bytes 12582916
  136.0 7.2 %copy-start.16 = (f32[8,256]{1,0:T(8,128)}, f32[8,256]{1,0:T(8,128)S(1)}, u32[]{:S(2)}) copy-start(f32[8,256]{1,0:T(8,128)S(1)} %get-tuple-element.85) | copy-start | bytes 24580
  136.0 9.1 %copy-start.10 = (f32[8,256]{1,0:T(8,128)}, f32[8,256]{1,0:T(8,128)S(1)}, u32[]{:S(2)}) copy-start(f32[8,256]{1,0:T(8,128)S(1)} %get-tuple-element.86) | copy-start | bytes 24580
  136.0 12.8 %copy-start.45 = (f32[8,256]{1,0:T(8,128)}, f32[8,256]{1,0:T(8,128)S(1)}, u32[]{:S(2)}) copy-start(f32[8,256]{1,0:T(8,128)S(1)} %get-tuple-element.84) | copy-start | bytes 24580
  138.7 4.6 copy-start.22
  138.7 6.4 %copy-start.19 = (f32[8,256]{1,0:T(8,128)}, f32[8,256]{1,0:T(8,128)S(1)}, u32[]{:S(2)}) copy-start(f32[8,256]{1,0:T(8,128)S(1)} %get-tuple-element.102) | copy-start | bytes 24580
  138.7 8.3 %copy-start.13 = (f32[8,256]{1,0:T(8,128)}, f32[8,256]{1,0:T(8,128)S(1)}, u32[]{:S(2)}) copy-start(f32[8,256]{1,0:T(8,128)S(1)} %get-tuple-element.103) | copy-start | bytes 24580
  138.7 4.6 copy-start.43
  143.2 1.9 copy-start.33
  143.2 1.9 copy-start.30
  143.2 3.8 copy-start.27
  143.3 1.9 copy-start.41
  145.2 1.8 copy-start.39
  147.0 1.9 copy-start.37
  150.7 5.8 %copy-start.7 = (bf16[1,256,8192]{2,1,0:T(8,128)(2,1)S(1)}, bf16[1,256,8192]{2,1,0:T(8,128)(2,1)}, u32[]{:S(2)}) copy-start(bf16[1,256,8192]{2,1,0:T(8,128)(2,1)} %param.6) | copy-start | bytes 12582916
  150.9 5.5 collective-permute-start.1
  164.6 369.7 %all-reduce.2.cloned.1.call-start = ((), (), s32[]{:S(2)}) async-start(), calls=%async_computation.3 | async-start | bytes 16777216 | tf_op jit(solution)/shard_map/psum | solution.py:151
  360.5 0.9 copy-start.9
  360.5 1.0 copy-start.17
  360.5 1.0 copy-start.23
  360.5 1.0 copy-start.34
  360.5 1.0 copy-start.44
  361.4 4.2 copy-start.3
  361.4 4.2 copy-start.11
  361.4 4.2 copy-start.20
  361.4 4.2 copy-start.31
  361.5 4.2 copy-start.42
  365.6 2.2 copy-start.1
  365.6 2.2 copy-start.14
  365.6 2.2 copy-start.28
  365.7 2.2 copy-start.40
  367.8 2.6 copy-start.5
  367.8 2.6 copy-start.26
  367.8 2.6 copy-start.38
  367.9 2.6 copy-start.46
  372.3 3.2 copy-start.18
  372.3 3.2 copy-start.24
  372.3 3.2 copy-start.35
  372.3 3.2 copy-start.12
  372.3 3.2 copy-start.21
  372.3 3.2 copy-start.32
  372.3 3.3 copy-start.15
  372.3 3.3 copy-start.29
Sparse Core Ops, SparseCore 0:
  9.5 106.6 all-gather.1
  164.7 195.7 reduce-scatter.1
  364.2 170.0 all-reduce.1
where the time goes:
time: 554 us
  waiting for transfers between devices  466 us (84%)
  matrix products  37.5 us (7%)
  other arithmetic  16.6 us (3%)
  local copies, waits for them, and re-layouts  15.8 us (3%)
  between operations  14.6 us (3%)
    reduce_scatter x1, waiting for transfers between devices, shards(): lax.psum_scatter(lax.dot_general(columns, key_grad_low, (((0,), (0,)), ((...  196 us
    psum x1, waiting for transfers between devices, shards(): summed = lax.psum(term_rows, ('seq', 'dp'))  158 us
    all_gather x1, waiting for transfers between devices, shards(): lax.all_gather(key_weight, 'fsdp', axis=0, tiled=True)  107 us
    unnamed x99, local copies, waits for them, and re-layouts  14.9 us
  transfers between devices with their start and end apart: 5, of which 4 were waited for; matrix products, arithmetic and copies ran while one was open for 3% of the time, Pallas kernels for 0%

commit v1 on v0

--- a/solution.py
+++ b/solution.py
@@ -148,7 +148,7 @@
         scatter_dimension=0,
         tiled=True,
     )
-    summed = lax.psum(term_rows, ("seq", "dp"))
+    summed = lax.psum(lax.psum(term_rows, "dp"), "seq")
     norm_factor = (seq_len * lax.axis_size("fsdp") * lax.axis_size("dp")) ** (-0.5)
     weight_grad = (summed * norm_factor).astype(jnp.bfloat16)
     return (

time: 554 us -> 828 us (1.49)
  waiting for transfers between devices: 466 us -> 739 us
    psum x1 -> x2, waiting for transfers between devices: 158 us -> 431 us  [shards(): summed = lax.psum(lax.psum(term_rows, 'dp'), 'seq')]
  transfers between devices with their start and end apart: 5 -> 6, of which waited for: 4 -> 5; matrix products, arithmetic and copies ran while one was open for 3% -> 2% of each run, Pallas kernels for 0% -> 0%
where the time goes in v1:
time: 828 us; the launch traced here: 827 us
  waiting for transfers between devices  739 us (89%)
  matrix products  37.5 us (5%)
  other arithmetic  16.6 us (2%)
  local copies, waits for them, and re-layouts  16.1 us (2%)
  between operations  14.6 us (2%)
    psum x2, waiting for transfers between devices, shards(): summed = lax.psum(lax.psum(term_rows, 'dp'), 'seq')  431 us
    reduce_scatter x1, waiting for transfers between devices, shards(): lax.psum_scatter(lax.dot_general(columns, key_grad_low, (((0,), (0,)), ((...  196 us
    all_gather x1, waiting for transfers between devices, shards(): lax.all_gather(key_weight, 'fsdp', axis=0, tiled=True)  107 us
  transfers between devices with their start and end apart: 6, of which 5 were waited for; matrix products, arithmetic and copies ran while one was open for 2% of the time, Pallas kernels for 0%

profile of v1, /device:TPU:0, one launch (start us, length us, event | category | flops | bytes accessed | tf_op | source)
XLA Modules:
  0.0 827.3 jit_solution(11839087837260096367)
XLA Ops:
  7.2 0.0 all-gather.2.cloned.1.call-start
  7.2 0.7 all-gather.2.cloned.1.call-update
  7.9 0.0 reduce-scatter.2.cloned.1.call-start
  8.0 0.2 reduce-window.8
  8.2 0.1 convert_reduce_fusion
  8.3 0.1 dynamic-slice_select_fusion
  8.3 0.6 convert_bitcast_fusion.3
  8.9 107.3 %all-gather.2.cloned.1.call-done = bf16[8192,512]{1,0:T(8,128)(2,1)} async-done(((bf16[4096,512]{1,0:T(8,128)(2,1)}), bf16[8192,512]{1,0:T(8,128)(2,1)}) %all-gather.2.cloned.1.call-update) | async-done | bytes 8388624 | tf_op jit(solution)/shard_map/all_gather | solution.py:113
  116.3 7.0 fusion.67
  123.3 1.6 collective-permute-start
  124.9 3.3 copy.58
  128.2 0.1 fusion.107
  128.3 0.0 collective-permute-done
  128.4 0.1 reshape.341
  128.5 0.8 fusion.113
  129.2 0.0 copy-start.8
  129.3 0.7 fusion.110
  130.0 0.0 copy-start.2
  130.0 0.7 fusion.111
  130.7 0.0 copy-start
  130.7 0.8 fusion.11
  131.5 0.9 fusion.4
  132.4 3.6 select_reduce_fusion.3
  136.0 2.6 fusion.6
  138.7 0.0 copy-start.22
  138.7 0.0 copy-start.19
  138.7 0.0 copy-start.13
  138.7 4.5 select_reduce_fusion.2
  143.2 0.0 copy-start.27
  143.3 1.8 fusion.97
  145.2 1.8 fusion.91
  147.0 1.8 fusion.85
  148.9 1.8 fusion.103
  150.7 0.0 copy-start.7
  150.7 0.1 pad_maximum_fusion.1
  150.8 0.1 fusion.112
  150.9 1.6 collective-permute-start.1
  152.5 3.9 collective-permute-done.1
  156.4 0.1 fusion.106
  156.5 8.1 convolution_bitcast_fusion
  164.6 0.0 reduce-scatter.2.cloned.1.call-update
  164.6 0.0 all-reduce.3.cloned.1.call-start
  164.6 195.8 %reduce-scatter.2.cloned.1.call-done = f32[4096,512]{0,1:T(8,128)} async-done(((f32[8192,512]{0,1:T(8,128)}), f32[4096,512]{0,1:T(8,128)}) %reduce-scatter.2.cloned.1.call-update) | async-done | bytes 8388624 | tf_op jit(solution)/shard_map/reduce_scatter | solution.py:143
  360.5 0.0 all-reduce.3.cloned.1.call-update
  360.5 0.3 all-reduce.5.cloned.1.call-start
  360.7 293.0 %all-reduce.3.cloned.1.call-done = f32[4096,512]{0,1:T(8,128)} async-done(((f32[4096,512]{0,1:T(8,128)}), f32[4096,512]{0,1:T(8,128)}) %all-reduce.3.cloned.1.call-update) | async-done | bytes 8388624 | tf_op jit(solution)/shard_map/psum | solution.py:151
  653.8 0.0 all-reduce.5.cloned.1.call-update
  653.8 0.9 copy-done.9
  654.8 4.1 fusion.58
  658.9 0.0 copy-done.3
  659.0 0.0 copy-start.1
  659.0 0.0 copy-start.28
  659.0 1.8 fusion.61
  660.8 1.1 copy-done.1
  661.9 1.8 fusion.64
  663.7 0.4 copy-done.5
  664.1 1.8 fusion.55
  665.9 0.0 copy-start.29
  665.9 0.3 pad_maximum_fusion
  666.2 2.9 copy.82
  669.2 0.6 maximum_bitcast_fusion
  669.8 138.2 %all-reduce.5.cloned.1.call-done = f32[4096,512]{0,1:T(8,128)} async-done(((f32[4096,512]{0,1:T(8,128)}), f32[4096,512]{0,1:T(8,128)}) %all-reduce.5.cloned.1.call-update) | async-done | bytes 8388624 | tf_op jit(solution)/shard_map/psum | solution.py:151
  808.0 6.4 multiply_convert_fusion
  814.3 6.4 copy.83
  (87 shorter events, 0.2 us)
Async XLA Ops:
  7.2 0.8 copy-start.47
  7.2 1.2 copy-start.36
  7.2 109.1 %all-gather.2.cloned.1.call-start = ((), (), s32[]{:S(2)}) async-start(), calls=%async_computation.1 | async-start | bytes 12582912 | tf_op jit(solution)/shard_map/all_gather | solution.py:113
  7.9 352.5 %reduce-scatter.2.cloned.1.call-start = ((), (), s32[]{:S(2)}) async-start(), calls=%async_computation.2 | async-start | bytes 25165824 | tf_op jit(solution)/shard_map/reduce_scatter | solution.py:143
  123.3 5.0 collective-permute-start
  129.2 3.1 copy-start.8
  130.0 15.2 %copy-start.2 = (f32[512,256,8]{1,0,2:T(8,128)}, f32[512,256,8]{1,0,2:T(8,128)S(1)}, u32[]{:S(2)}) copy-start(f32[512,256,8]{1,0,2:T(8,128)S(1)} %fusion.110) | copy-start | bytes 12582916
  130.7 16.3 %copy-start = (f32[512,256,8]{1,0,2:T(8,128)}, f32[512,256,8]{1,0,2:T(8,128)S(1)}, u32[]{:S(2)}) copy-start(f32[512,256,8]{1,0,2:T(8,128)S(1)} %fusion.111) | copy-start | bytes 12582916
  131.5 17.4 %copy-start.4 = (f32[512,256,8]{1,0,2:T(8,128)}, f32[512,256,8]{1,0,2:T(8,128)S(1)}, u32[]{:S(2)}) copy-start(f32[512,256,8]{1,0,2:T(8,128)S(1)} %get-tuple-element.127) | copy-start | bytes 12582916
  132.4 16.5 %copy-start.25 = (f32[8,256]{1,0:T(8,128)}, f32[8,256]{1,0:T(8,128)S(1)}, u32[]{:S(2)}) copy-start(f32[8,256]{1,0:T(8,128)S(1)} %fusion.4) | copy-start | bytes 24580
  136.0 7.2 copy-start.6
  136.0 7.2 copy-start.16
  136.0 9.1 %copy-start.10 = (f32[8,256]{1,0:T(8,128)}, f32[8,256]{1,0:T(8,128)S(1)}, u32[]{:S(2)}) copy-start(f32[8,256]{1,0:T(8,128)S(1)} %get-tuple-element.86) | copy-start | bytes 24580
  136.0 12.8 %copy-start.45 = (f32[8,256]{1,0:T(8,128)}, f32[8,256]{1,0:T(8,128)S(1)}, u32[]{:S(2)}) copy-start(f32[8,256]{1,0:T(8,128)S(1)} %get-tuple-element.84) | copy-start | bytes 24580
  138.7 4.6 copy-start.22
  138.7 6.4 copy-start.19
  138.7 8.3 %copy-start.13 = (f32[8,256]{1,0:T(8,128)}, f32[8,256]{1,0:T(8,128)S(1)}, u32[]{:S(2)}) copy-start(f32[8,256]{1,0:T(8,128)S(1)} %get-tuple-element.103) | copy-start | bytes 24580
  138.7 4.6 copy-start.43
  143.2 1.9 copy-start.33
  143.2 1.9 copy-start.30
  143.2 3.8 copy-start.27
  143.3 1.9 copy-start.41
  145.2 1.8 copy-start.39
  147.0 1.9 copy-start.37
  150.7 5.8 copy-start.7
  150.9 5.5 collective-permute-start.1
  164.6 489.2 %all-reduce.3.cloned.1.call-start = ((), (), s32[]{:S(2)}) async-start(), calls=%async_computation.3 | async-start | bytes 16777216 | tf_op jit(solution)/shard_map/psum | solution.py:151
  360.5 447.5 %all-reduce.5.cloned.1.call-start = ((), (), s32[]{:S(2)}) async-start(), calls=%async_computation.4 | async-start | bytes 16777216 | tf_op jit(solution)/shard_map/psum | solution.py:151
  653.8 0.9 copy-start.9
  653.8 1.0 copy-start.17
  653.8 1.0 copy-start.23
  653.8 1.0 copy-start.34
  653.8 1.0 copy-start.44
  654.7 4.2 copy-start.3
  654.8 4.2 copy-start.11
  654.8 4.2 copy-start.20
  654.8 4.2 copy-start.31
  654.8 4.2 copy-start.42
  659.0 2.9 copy-start.1
  659.0 2.9 copy-start.14
  659.0 2.9 copy-start.28
  659.0 2.9 copy-start.40
  661.9 2.2 copy-start.5
  661.9 2.2 copy-start.26
  661.9 2.2 copy-start.38
  661.9 2.2 copy-start.46
  665.8 3.2 copy-start.18
  665.8 3.2 copy-start.24
  665.9 3.2 copy-start.35
  665.9 3.2 copy-start.12
  665.9 3.2 copy-start.21
  665.9 3.2 copy-start.32
  665.9 3.3 copy-start.15
  665.9 3.3 copy-start.29
Sparse Core Ops, SparseCore 0:
  9.5 106.6 all-gather.1
  164.7 195.7 reduce-scatter.1
  362.9 290.8 all-reduce.2
  656.1 151.8 all-reduce.4
